TPU v7x, 32 devices: a whole 2x2x4 slice. The times are simulated.
32 devices in a mesh: grp: 2 (over y), patch: 8 (over z, x), frame: 2 (over core).
Axes of the slice: x: 2, y: 2, z: 4, core: 2. Of those that a mesh axis runs over, the one named last changes fastest.
Arguments:
- video_tokens: bfloat16 [4, 16, 80, 1152], P('grp', 'frame', 'patch'), parts along dimension 0, may hold values from -6 to 6
- timestep: int32 [2], P('grp'), parts along dimension 0, may hold values from 0 to 999
- w_qkv: bfloat16 [2, 1152, 1728], P(None, 'patch'), may hold values from -0.1875 to 0.1875
- w_out: bfloat16 [2, 576, 1152], P(None, None, 'patch'), may hold values from -0.25 to 0.25
- qk_gain: float32 [2, 2, 72], replicated, may hold values from 1 to 2.5
- mod_table: float32 [2, 3, 1152], replicated, may hold values from -3 to 3
- mod_gain: float32 [2, 3, 1152], replicated, may hold values from -3 to 3
Outputs:
- denoised: bfloat16 [4, 16, 80, 1152], P('grp', 'frame', 'patch'), parts along dimension 0
There are 2 independent parts, one for each index of `grp`. A program takes and returns all parts, laid end to end along the dimension named above; an argument that names none is the same for every part. Nothing has to cross between parts.
All inputs are finite; a program needn't handle non-finite values.
Results may differ from a plain program's by a relative error of at most 0.013.
Values may be sent and summed in bfloat16 or wider, within the bound.
A program may use at most 128 MiB of HBM per device.

v0:
```python
import math

import jax
import jax.numpy as jnp
from jax import lax
from jax.sharding import PartitionSpec as P


def time_embed(timestep, width):
    half_width = width // 2
    freqs = jnp.exp(-math.log(10000.0) * jnp.arange(half_width, dtype=jnp.float32) / half_width)
    angles = timestep[0].astype(jnp.float32) * freqs
    return jnp.concatenate([jnp.cos(angles), jnp.sin(angles)])


def modulate(tokens, table, gains, embed):
    params = table + gains * embed[None, :]
    values = tokens.astype(jnp.float32)
    centre = jnp.mean(values, axis=-1, keepdims=True)
    centred = values - centre
    spread = jnp.mean(centred * centred, axis=-1, keepdims=True)
    normed = centred * lax.rsqrt(spread + 1e-06)
    return ((normed * (1.0 + params[1]) + params[0]).astype(jnp.bfloat16), params[2])


def head_norm(values, gain):
    meansq = jnp.mean(values * values, axis=-1, keepdims=True)
    return (values * lax.rsqrt(meansq + 1e-06) * gain).astype(jnp.bfloat16)


def fetch_weights(qkv_rows, out_cols):
    return (
        lax.all_gather(qkv_rows, "patch", axis=0, tiled=True),
        lax.all_gather(out_cols, "patch", axis=1, tiled=True),
    )


def attend_items(stacked):
    head_size = stacked.shape[-1]
    query = stacked[0, 0]
    key = stacked[1, 0]
    value = stacked[2, 0]
    scores = jnp.einsum("nqd,nkd->nqk", query, key, preferred_element_type=jnp.float32) / math.sqrt(
        head_size
    )
    raised = jnp.exp(scores)
    total = jnp.sum(raised, axis=-1, keepdims=True)
    summed = jnp.einsum(
        "nqk,nkd->nqd", raised.astype(jnp.bfloat16), value, preferred_element_type=jnp.float32
    )
    return (summed / total).astype(jnp.bfloat16)[None]


def spatial(query, key, value, videos, fr_dev, patch_dev):
    rows, heads, head_size = query.shape
    groups = lax.axis_size("patch")
    per_group = videos * fr_dev * heads // groups
    stacked = jnp.stack([query, key, value])
    stacked = stacked.reshape(3, videos * fr_dev, patch_dev, heads, head_size)
    stacked = stacked.transpose(0, 1, 3, 2, 4).reshape(3, groups, per_group, patch_dev, head_size)
    attended = attend_items(
        lax.all_to_all(stacked, "patch", split_axis=1, concat_axis=3, tiled=True)
    )
    returned = lax.all_to_all(attended, "patch", split_axis=2, concat_axis=0, tiled=True)
    returned = returned.reshape(videos * fr_dev, heads, patch_dev, head_size).transpose(0, 2, 1, 3)
    return returned.reshape(rows, heads * head_size)


def frame_attend(query, key, value, heads):
    videos, q_frames, patches, feat = query.shape
    k_frames = key.shape[1]
    head_size = feat // heads
    query = query.reshape(videos, q_frames, patches, heads, head_size)
    key = key.reshape(videos, k_frames, patches, heads, head_size)
    value = value.reshape(videos, k_frames, patches, heads, head_size)
    scores = jnp.einsum(
        "bfphd,bgphd->bphfg", query, key, preferred_element_type=jnp.float32
    ) / math.sqrt(head_size)
    raised = jnp.exp(scores)
    total = jnp.sum(raised, axis=-1)
    summed = jnp.einsum(
        "bphfg,bgphd->bfphd", raised.astype(jnp.bfloat16), value, preferred_element_type=jnp.float32
    )
    result = summed / total.transpose(0, 3, 1, 2)[..., None]
    return result.astype(jnp.bfloat16).reshape(videos, q_frames, patches, feat)


def temporal(query, key, value, videos, fr_dev, patch_dev):
    rows, heads, head_size = query.shape
    feat = heads * head_size
    query4 = query.reshape(videos, fr_dev, patch_dev, feat)
    key4 = key.reshape(videos, fr_dev, patch_dev, feat)
    value4 = value.reshape(videos, fr_dev, patch_dev, feat)
    joined = jnp.concatenate([query4, key4, value4], axis=3)
    swapped = lax.all_to_all(joined, "frame", split_axis=2, concat_axis=1, tiled=True)
    result = frame_attend(
        swapped[..., :feat], swapped[..., feat : 2 * feat], swapped[..., 2 * feat :], heads
    )
    returned = lax.all_to_all(result, "frame", split_axis=1, concat_axis=2, tiled=True)
    return returned.reshape(rows, feat)


def per_device(video_tokens, timestep, w_qkv, w_out, qk_gain, mod_table, mod_gain):
    videos, fr_dev, patch_dev, width = video_tokens.shape
    rows = videos * fr_dev * patch_dev
    head_size = qk_gain.shape[2]
    heads = w_out.shape[1] // head_size
    embed = time_embed(timestep, width)
    tokens = video_tokens.reshape(rows, width)
    for layer in range(2):
        qkv_full, out_full = fetch_weights(w_qkv[layer], w_out[layer])
        mixed, gate = modulate(tokens, mod_table[layer], mod_gain[layer], embed)
        joint = jnp.dot(mixed, qkv_full, preferred_element_type=jnp.float32)
        joint = joint.reshape(rows, 3, heads, head_size)
        query = head_norm(joint[:, 0], qk_gain[layer, 0])
        key = head_norm(joint[:, 1], qk_gain[layer, 1])
        value = joint[:, 2].astype(jnp.bfloat16)
        if layer == 0:
            attended = spatial(query, key, value, videos, fr_dev, patch_dev)
        else:
            attended = temporal(query, key, value, videos, fr_dev, patch_dev)
        update = jnp.dot(attended, out_full, preferred_element_type=jnp.float32)
        tokens = (tokens.astype(jnp.float32) + gate * update).astype(jnp.bfloat16)
    return tokens.reshape(videos, fr_dev, patch_dev, width)


def solution(mesh):
    placed = (
        P("grp", "frame", "patch", None),
        P("grp"),
        P(None, "patch", None),
        P(None, None, "patch"),
        P(),
        P(),
        P(),
    )
    return jax.shard_map(
        per_device,
        mesh=mesh,
        in_specs=placed,
        out_specs=P("grp", "frame", "patch", None),
        check_vma=False,
    )
```

profile of v0, /device:TPU:0, one launch (start us, length us, event | category | flops | bytes accessed | tf_op | source)
XLA Modules:
  0.0 268.2 jit_solution(7167278873392558477)
XLA Ops:
  6.6 2.3 fusion.36
  9.0 0.8 fusion.39
  12.4 72.5 %all-gather.9.cloned.1.call-done = bf16[1,1152,1728]{2,1,0:T(8,128)(2,1)} async-done(((bf16[1,144,1728]{2,1,0:T(8,128)(2,1)}), bf16[1,1152,1728]{2,1,0:T(8,128)(2,1)}) %all-gather.9.cloned.1.call-update) | async-done | bytes 3981328 | tf_op jit(solution)/shard_map/all_gather | solution.py:33
  84.8 6.5 %copy.88 = bf16[1728,1152]{1,0:T(8,128)(2,1)} copy(bf16[1728,1152]{0,1:T(8,128)(2,1)} %bitcast.115) | data formatting | bytes 7962624 | tf_op jit(solution)/shard_map/dot_general | solution.py:113
  91.4 3.6 %fusion.15 = f32[160,3,8,72]{0,3,2,1:T(8,128)S(1)} fusion(bf16[3,8,72,1152]{3,2,1,0:T(8,128)(2,1)} %bitcast.116, bf16[160,1152,1,1]{1,0,2,3:T(8,128)(2,1)S(1)} %reshape.231), kind=kOutput, calls=%fused_computation.38 | convolution fusion | flops 637009920 | bytes 5455872 | tf_op jit(solution)/shard_map/dot_general | solution.py:113
  97.8 40.4 %all_to_all.63 = bf16[3,8,16,10,72]{4,2,3,0,1:T(8,128)(2,1)S(1)} all-to-all(bf16[3,8,16,10,72]{4,2,3,0,1:T(8,128)(2,1)S(1)} %copy.95), channel_id=1, replica_groups=mesh['grp'=2,'patch'=8,'frame'=2] {'patch'}, dimensions={1} | all-to-all | bytes 1105920 | tf_op jit(solution)/shard_map/all_to_all | solution.py:62
  139.1 1.0 copy.100
  140.1 3.7 %all-to-all-start.1 = ((bf16[1,16,80,72]{3,1,0,2:T(8,128)(2,1)}), bf16[1,16,80,72]{3,1,0,2:T(8,128)(2,1)S(1)}, u32[]{:S(2)}, u32[]{:S(2)}) async-start(bf16[1,16,80,72]{3,1,0,2:T(8,128)(2,1)} %copy.100), calls=%async_computation.1 | async-start | bytes 655360 | tf_op jit(solution)/shard_map/all_to_all | solution.py:64
  144.7 15.2 %all-to-all-done.1 = bf16[1,16,80,72]{3,1,0,2:T(8,128)(2,1)S(1)} async-done(((bf16[1,16,80,72]{3,1,0,2:T(8,128)(2,1)}), bf16[1,16,80,72]{3,1,0,2:T(8,128)(2,1)S(1)}, u32[]{:S(2)}, u32[]{:S(2)}) %all-to-all-start.1) | async-done | bytes 184352 | tf_op jit(solution)/shard_map/all_to_all | solution.py:64
  160.3 2.1 fusion.43
  162.6 52.2 %all-gather.13.cloned.1.call-done = bf16[1,1152,1728]{2,1,0:T(8,128)(2,1)} async-done(((bf16[1,144,1728]{2,1,0:T(8,128)(2,1)}), bf16[1,1152,1728]{2,1,0:T(8,128)(2,1)}) %all-gather.13.cloned.1.call-update) | async-done | bytes 3981328 | tf_op jit(solution)/shard_map/all_gather | solution.py:33
  214.8 4.2 %fusion = f32[160,1728]{1,0:T(8,128)} fusion(bf16[1,1152,1728]{2,1,0:T(8,128)(2,1)} %all-gather.13.cloned.1.call-done, f32[160,1152]{1,0:T(8,128)S(1)} %get-tuple-element.42, f32[1152]{0:T(1024)S(1)} %get-tuple-element.10, f32[1152]{0:T(1024)S(1)} %get-tuple-element.11, f32[160]{0:T(256)S(1)} %add_rsqrt_fusion.5, f32[160]{0:T(256)S(1)} %broadcast_multiply_fusion.1), kind=kOutput, calls=%fused_computation | convolution fusion | flops 637931520 | bytes 5835008 | tf_op jit(solution)/shard_map/dot_general | solution.py:113
  219.0 2.2 reshape.219
  222.0 1.1 multiply_reduce_fusion.2
  224.9 1.4 squeeze.62
  226.2 2.1 convert_element_type.113
  228.3 0.8 multiply_convert_fusion
  229.1 0.8 multiply_convert_fusion.1
  230.1 1.4 concatenate.8
  231.6 4.2 %all_to_all.64 = bf16[2,8,10,1728]{3,1,0,2:T(8,128)(2,1)S(1)} all-to-all(bf16[2,8,10,1728]{3,1,0,2:T(8,128)(2,1)S(1)} %copy.108), channel_id=1, replica_groups=mesh['grp'=2,'patch'=8,'frame'=2] {'frame'}, dimensions={2} | all-to-all | bytes 1105920 | tf_op jit(solution)/shard_map/all_to_all | solution.py:95
  238.5 3.9 %all_to_all.65 = bf16[2,16,5,576]{3,0,2,1:T(2,128)(2,1)S(1)} all-to-all(bf16[2,16,5,576]{3,0,2,1:T(2,128)(2,1)S(1)} %reshape.233), channel_id=1, replica_groups=mesh['grp'=2,'patch'=8,'frame'=2] {'frame'}, dimensions={1} | all-to-all | bytes 368640 | tf_op jit(solution)/shard_map/all_to_all | solution.py:99
  242.5 16.2 %all-gather.15.cloned.1.call-done = bf16[1,576,1152]{1,2,0:T(8,128)(2,1)} async-done(((bf16[1,576,144]{1,2,0:T(8,128)(2,1)}), bf16[1,576,1152]{1,2,0:T(8,128)(2,1)}) %all-gather.15.cloned.1.call-update) | async-done | bytes 1327120 | tf_op jit(solution)/shard_map/all_gather | solution.py:34
  258.8 2.0 fusion.6
  260.9 0.8 copy.118
  (91 shorter events, 12.9 us)
Async XLA Ops:
  6.5 2.4 copy-start.2
  6.5 4.8 %copy-start.4 = (f32[2,3,1152]{2,0,1:T(2,128)S(1)}, f32[2,3,1152]{2,0,1:T(2,128)}, u32[]{:S(2)}) copy-start(f32[2,3,1152]{2,0,1:T(2,128)} %param.12) | copy-start | bytes 82948
  6.5 4.8 %copy-start.3 = (f32[2,3,1152]{2,0,1:T(2,128)S(1)}, f32[2,3,1152]{2,0,1:T(2,128)}, u32[]{:S(2)}) copy-start(f32[2,3,1152]{2,0,1:T(2,128)} %param.13) | copy-start | bytes 82948
  6.5 4.9 %copy-start = (bf16[2,8,10,1152]{3,1,2,0:T(8,128)(2,1)S(1)}, bf16[2,8,10,1152]{3,1,2,0:T(8,128)(2,1)}, u32[]{:S(2)}) copy-start(bf16[2,8,10,1152]{3,1,2,0:T(8,128)(2,1)} %param.7) | copy-start | bytes 1105924
  6.5 78.3 %all-gather.9.cloned.1.call-start = ((), (), s32[]{:S(2)}) async-start(), calls=%async_computation.4 | async-start | bytes 4644864 | tf_op jit(solution)/shard_map/all_gather | solution.py:33
  8.9 151.4 %all-gather.11.cloned.1.call-start = ((), (), s32[]{:S(2)}) async-start(), calls=%async_computation.5 | async-start | bytes 1658880 | tf_op jit(solution)/shard_map/all_gather | solution.py:34
  9.8 205.1 %all-gather.13.cloned.1.call-start = ((), (), s32[]{:S(2)}) async-start(), calls=%async_computation.6 | async-start | bytes 4644864 | tf_op jit(solution)/shard_map/all_gather | solution.py:33
  11.4 0.9 copy-start.5
  140.1 19.9 %all-to-all-start.1 = ((bf16[1,16,80,72]{3,1,0,2:T(8,128)(2,1)}), bf16[1,16,80,72]{3,1,0,2:T(8,128)(2,1)S(1)}, u32[]{:S(2)}, u32[]{:S(2)}) async-start(bf16[1,16,80,72]{3,1,0,2:T(8,128)(2,1)} %copy.100), calls=%async_computation.1 | async-start | bytes 655360 | tf_op jit(solution)/shard_map/all_to_all | solution.py:64
  143.7 115.0 %all-gather.15.cloned.1.call-start = ((), (), s32[]{:S(2)}) async-start(), calls=%async_computation.7 | async-start | bytes 1658880 | tf_op jit(solution)/shard_map/all_gather | solution.py:34
  229.1 1.0 copy-start.1
Sparse Core Ops, SparseCore 0:
  9.6 75.2 all-gather.8
  87.0 51.2 all-gather.10
  140.5 74.2 all-gather.12
  216.9 41.8 all-gather.14
where the time goes:
time: 269 us; the launch traced here: 268 us
  waiting for transfers between devices  157 us (58%)
  blocking collectives  48.4 us (18%)
  local copies, waits for them, and re-layouts  26.3 us (10%)
  between operations  14.2 us (5%)
  matrix products  13.3 us (5%)
  other arithmetic  4.76 us (2%)
  starting transfers between devices  4 us (1%)
    all_gather x2, waiting for transfers between devices, fetch_weights(): lax.all_gather(qkv_rows, 'patch', axis=0, tiled=True)  125 us
    all_to_all x1, blocking collectives, spatial(): lax.all_to_all(stacked, 'patch', split_axis=1, concat_axis=3, tiled=True)  40.4 us
    all_gather x2, waiting for transfers between devices, fetch_weights(): lax.all_gather(out_cols, 'patch', axis=1, tiled=True)  16.3 us
    all_to_all x1, waiting for transfers between devices, spatial(): lax.all_to_all(attended, 'patch', split_axis=2, concat_axis=0, tiled=True)  15.2 us
    dot_general x2, matrix products, per_device(): joint = jnp.dot(mixed, qkv_full, preferred_element_type=jnp.float32)  7.8 us
    dot_general x1, local copies, waits for them, and re-layouts, per_device(): joint = jnp.dot(mixed, qkv_full, preferred_element_type=jnp.float32)  6.5 us
  transfers between devices with their start and end apart: 5, of which 4 were waited for; matrix products, arithmetic and copies ran while one was open for 15% of the time, Pallas kernels for 0%

commit v1 on v0

--- a/solution.py
+++ b/solution.py
@@ -1,8 +1,12 @@
+import functools
 import math
 
 import jax
 import jax.numpy as jnp
+import numpy as np
 from jax import lax
+from jax.experimental import pallas as pl
+from jax.experimental.pallas import tpu as pltpu
 from jax.sharding import PartitionSpec as P
 
 
@@ -124,6 +128,356 @@
     return tokens.reshape(videos, fr_dev, patch_dev, width)
 
 
+MESH = pl.DeviceIdType.MESH
+CHUNKS = 3
+HIGHEST = lax.Precision.HIGHEST
+
+
+def dot_f32(a, b, contract):
+    return lax.dot_general(
+        a, b, ((contract[:1], contract[1:]), ((), ())), preferred_element_type=jnp.float32
+    )
+
+
+def ring_to_patch(pos, count):
+    upper = lax.div(pos, count // 2)
+    return (1 - upper) * 2 * pos + upper * (2 * count - 1 - 2 * pos)
+
+
+def patch_to_ring(patch, count):
+    side = lax.rem(patch, 2)
+    level = lax.div(patch, 2)
+    return (1 - side) * level + side * (count - 1 - level)
+
+
+def norm_tokens(values, params):
+    centre = jnp.mean(values, axis=-1, keepdims=True)
+    centred = values - centre
+    spread = jnp.mean(centred * centred, axis=-1, keepdims=True)
+    normed = centred * lax.rsqrt(spread + 1e-06)
+    return (normed * (1.0 + params[1:2]) + params[0:1]).astype(jnp.bfloat16)
+
+
+def norm_heads(values, gain, heads_map, head_size):
+    total = lax.dot_general(
+        values * values,
+        heads_map,
+        (((1,), (1,)), ((), ())),
+        precision=HIGHEST,
+        preferred_element_type=jnp.float32,
+    )
+    scale = lax.rsqrt(total / head_size + 1e-06)
+    wide = lax.dot_general(
+        scale,
+        heads_map,
+        (((1,), (0,)), ((), ())),
+        precision=HIGHEST,
+        preferred_element_type=jnp.float32,
+    )
+    return (values * wide * gain).astype(jnp.bfloat16)
+
+
+def attend_heads(query, key, value, heads_map, mask, att_ref, head_size):
+    feat = query.shape[1]
+    att_ref[...] = jnp.zeros_like(att_ref)
+    for head in range(feat // head_size):
+        low = head * head_size // 128 * 128
+        high = min(-(-(head + 1) * head_size // 128) * 128, feat)
+        lanes = heads_map[head : head + 1, low:high].astype(jnp.bfloat16)
+        scores = dot_f32(query[:, low:high] * lanes, key[:, low:high], (1, 1))
+        raised = jnp.where(mask > 0.0, jnp.exp(scores / math.sqrt(head_size)), 0.0)
+        total = jnp.sum(raised, axis=-1, keepdims=True)
+        summed = dot_f32(raised.astype(jnp.bfloat16), value[:, low:high] * lanes, (1, 0))
+        att_ref[:, low:high] += summed / total
+    return att_ref[...].astype(jnp.bfloat16)
+
+
+def fused_kernel(
+    head_size, x_ref, w_ref, par_ref, gain_ref, heads_ref, mask_ref, out_ref,
+    wbuf, xin, mid_send, mid_recv, xf, att, res,
+    local_sem, in_send, in_recv, ring_send, ring_recv, sib_send, sib_recv,
+    mid_ssem, mid_rsem, fin_send, fin_recv,
+):
+    videos, fr_dev, patch_dev, width = x_ref.shape
+    layers, rows, lanes = w_ref.shape
+    count = fr_dev
+    half = lanes // 2
+    feat = heads_ref.shape[1]
+    grp = lax.axis_index("grp")
+    me = lax.axis_index("patch")
+    core = lax.axis_index("frame")
+    sib = 1 - core
+    pos = patch_to_ring(me, count)
+    turn = 1 - 2 * core
+    piece = rows // CHUNKS
+    onward = ring_to_patch(lax.rem(pos + turn + count, count), count)
+
+    barrier = pltpu.get_barrier_semaphore()
+    for k in range(count):
+        for s in range(2):
+            if k or s:
+                pl.semaphore_signal(
+                    barrier,
+                    inc=1,
+                    device_id=(grp, lax.rem(me + k, count), lax.rem(core + s, 2)),
+                    device_id_type=MESH,
+                )
+    pl.semaphore_wait(barrier, 2 * count - 1)
+
+    def remote(src, dst, send_sem, recv_sem, patch, frame):
+        return pltpu.make_async_remote_copy(
+            src_ref=src,
+            dst_ref=dst,
+            send_sem=send_sem,
+            recv_sem=recv_sem,
+            device_id=(grp, patch, frame),
+            device_id_type=MESH,
+        )
+
+    own_in = pltpu.make_async_copy(x_ref.at[:, me], xin.at[me], local_sem.at[0])
+    own_w = pltpu.make_async_copy(
+        w_ref, wbuf.at[:, pl.ds(pl.multiple_of(me * rows, 16), rows), :], local_sem.at[1]
+    )
+    own_in.start()
+    sent = []
+    for k in range(1, count):
+        peer = lax.rem(me + k, count)
+        copy = remote(x_ref.at[:, peer], xin.at[me], in_send.at[k], in_recv.at[me], peer, core)
+        copy.start()
+        sent.append(copy)
+
+    def block(layer, step, chunk, owner_core, from_input):
+        direction = 1 - 2 * owner_core
+        source = ring_to_patch(lax.rem(pos - direction * step + count, count), count)
+        columns = pl.ds(pl.multiple_of(owner_core * half, 128), half)
+        if from_input:
+            return w_ref.at[layer, pl.ds(chunk * piece, piece), columns]
+        start = pl.multiple_of(source * rows + chunk * piece, 16)
+        return wbuf.at[layer, pl.ds(start, piece), columns]
+
+    def ring_copy(layer, step, chunk):
+        return remote(
+            block(layer, step, chunk, core, step == 0),
+            block(layer, step, chunk, core, False),
+            ring_send.at[layer, step, chunk],
+            ring_recv.at[layer, step, chunk],
+            onward,
+            core,
+        )
+
+    def arrived(layer, step, chunk):
+        landed = block(layer, step + 1, chunk, core, False)
+        remote(
+            landed,
+            landed,
+            ring_send.at[layer, step, chunk],
+            ring_recv.at[layer, step, chunk],
+            onward,
+            core,
+        ).wait_recv()
+        if step + 1 < count - 1:
+            copy = ring_copy(layer, step + 1, chunk)
+            copy.start()
+            sent.append(copy)
+        copy = remote(
+            landed,
+            landed,
+            sib_send.at[layer, step, chunk],
+            sib_recv.at[layer, step, chunk],
+            me,
+            sib,
+        )
+        copy.start()
+        sent.append(copy)
+
+    def ring_step(layer, step):
+        for chunk in range(CHUNKS):
+            arrived(layer, step, chunk)
+
+    def sibling_done(layer):
+        for step in range(count - 1):
+            for chunk in range(CHUNKS):
+                landed = block(layer, step + 1, chunk, sib, False)
+                remote(
+                    landed,
+                    landed,
+                    sib_send.at[layer, step, chunk],
+                    sib_recv.at[layer, step, chunk],
+                    me,
+                    sib,
+                ).wait_recv()
+
+    for layer in range(layers):
+        for chunk in range(CHUNKS):
+            copy = ring_copy(layer, 0, chunk)
+            copy.start()
+            sent.append(copy)
+    own_w.start()
+
+    heads_map = heads_ref[...]
+
+    def project(layer, mixed):
+        joint = jnp.dot(mixed, wbuf[layer, :, : 3 * feat], preferred_element_type=jnp.float32)
+        query = norm_heads(joint[:, :feat], gain_ref[layer, 0:1], heads_map, head_size)
+        key = norm_heads(joint[:, feat : 2 * feat], gain_ref[layer, 1:2], heads_map, head_size)
+        return query, key, joint[:, 2 * feat :].astype(jnp.bfloat16)
+
+    def update(layer, tokens, attended):
+        added = dot_f32(attended, wbuf[layer, :, 3 * feat :], (1, 1))
+        return tokens + par_ref[layer, 2:3] * added
+
+    own_in.wait()
+    for k in range(1, count):
+        peer = lax.rem(me + k, count)
+        remote(
+            xin.at[peer], xin.at[peer], in_send.at[k], in_recv.at[peer], peer, core
+        ).wait_recv()
+    for video in range(videos):
+        for patch in range(count):
+            low = (video * count + patch) * patch_dev
+            xf[low : low + patch_dev, :] = xin[patch, video].astype(jnp.float32)
+    mixed = norm_tokens(xf[...], par_ref[0])
+    for step in range(count - 1):
+        ring_step(0, step)
+    own_w.wait()
+    sibling_done(0)
+    query, key, value = project(0, mixed)
+    ring_step(1, 0)
+    attended = attend_heads(query, key, value, heads_map, mask_ref[0], att, head_size)
+    ring_step(1, 1)
+    xf[...] = update(0, xf[...], attended)
+
+    frame = core * count + me
+    for k in range(2 * count):
+        video, patch = k // count, k % count
+        low = k * patch_dev
+        mid_send[k] = xf[low : low + patch_dev, :].astype(jnp.bfloat16)
+    own_mid = pltpu.make_async_copy(mid_send.at[frame], mid_recv.at[frame], local_sem.at[2])
+    own_mid.start()
+    for s in range(2):
+        for k in range(count):
+            if k or s:
+                peer, video = lax.rem(me + k, count), lax.rem(core + s, 2)
+                copy = remote(
+                    mid_send.at[video * count + peer],
+                    mid_recv.at[frame],
+                    mid_ssem.at[s * count + k],
+                    mid_rsem.at[frame],
+                    peer,
+                    video,
+                )
+                copy.start()
+                sent.append(copy)
+    for step in range(2, count - 1):
+        ring_step(1, step)
+    own_mid.wait()
+    for s in range(2):
+        for k in range(count):
+            if k or s:
+                peer, video = lax.rem(me + k, count), lax.rem(core + s, 2)
+                landed = mid_recv.at[video * count + peer]
+                remote(
+                    landed,
+                    landed,
+                    mid_ssem.at[s * count + k],
+                    mid_rsem.at[video * count + peer],
+                    peer,
+                    video,
+                ).wait_recv()
+
+    for k in range(2 * count):
+        low = k * patch_dev
+        xf[low : low + patch_dev, :] = mid_recv[k].astype(jnp.float32)
+    mixed = norm_tokens(xf[...], par_ref[1])
+    sibling_done(1)
+    query, key, value = project(1, mixed)
+    attended = attend_heads(query, key, value, heads_map, mask_ref[1], att, head_size)
+    xf[...] = update(1, xf[...], attended)
+    for k in range(2 * count):
+        low = k * patch_dev
+        res[k] = xf[low : low + patch_dev, :].astype(jnp.bfloat16)
+    own_out = pltpu.make_async_copy(
+        res.at[pl.ds(core * count, count)], out_ref.at[core], local_sem.at[3]
+    )
+    own_out.start()
+    final = remote(
+        res.at[pl.ds(sib * count, count)], out_ref.at[core], fin_send, fin_recv, me, sib
+    )
+    final.start()
+    own_out.wait()
+    final.wait_send()
+    remote(
+        out_ref.at[sib], out_ref.at[sib], fin_send, fin_recv, me, sib
+    ).wait_recv()
+    for copy in sent:
+        copy.wait_send()
+
+
+def fused_device(video_tokens, timestep, w_qkv, w_out, qk_gain, mod_table, mod_gain):
+    videos, fr_dev, patch_dev, width = video_tokens.shape
+    layers, rows, _ = w_qkv.shape
+    head_size = qk_gain.shape[2]
+    feat = w_out.shape[1]
+    heads = feat // head_size
+    tokens = videos * fr_dev * patch_dev
+    embed = time_embed(timestep, width)
+    params = mod_table + mod_gain * embed[None, None, :]
+    gains = jnp.tile(qk_gain, (1, 1, heads))
+    joined = jnp.concatenate([w_qkv, w_out.transpose(0, 2, 1)], axis=2)
+    lanes = joined.shape[2]
+    heads_map = jnp.asarray(np.repeat(np.eye(heads, dtype=np.float32), head_size, axis=1))
+    row = np.arange(tokens)
+    frame_patches = tokens // videos
+    masks = np.stack(
+        [
+            (row[:, None] // frame_patches) == (row[None, :] // frame_patches),
+            (row[:, None] % patch_dev) == (row[None, :] % patch_dev),
+        ]
+    ).astype(np.float32)
+    vmem = pl.BlockSpec(memory_space=pltpu.VMEM)
+    count = fr_dev
+    bf16, f32 = jnp.bfloat16, jnp.float32
+    dma = pltpu.SemaphoreType.DMA
+    ring = (layers, count - 1, CHUNKS)
+    return pl.pallas_call(
+        functools.partial(fused_kernel, head_size),
+        out_shape=jax.ShapeDtypeStruct(video_tokens.shape, bf16),
+        in_specs=[vmem] * 6,
+        out_specs=vmem,
+        scratch_shapes=[
+            pltpu.VMEM((layers, count * rows, lanes), bf16),
+            pltpu.VMEM((count, videos, patch_dev, width), bf16),
+            pltpu.VMEM((2 * count, patch_dev, width), bf16),
+            pltpu.VMEM((2 * count, patch_dev, width), bf16),
+            pltpu.VMEM((tokens, width), f32),
+            pltpu.VMEM((tokens, feat), f32),
+            pltpu.VMEM((2 * count, patch_dev, width), bf16),
+            dma((4,)),
+            dma((count,)),
+            dma((count,)),
+            dma(ring),
+            dma(ring),
+            dma(ring),
+            dma(ring),
+            dma((2 * count,)),
+            dma((2 * count,)),
+            dma,
+            dma,
+        ],
+        compiler_params=pltpu.CompilerParams(
+            collective_id=0, has_side_effects=True, vmem_limit_bytes=56 * 1024 * 1024
+        ),
+        name="blocks",
+    )(video_tokens, joined, params, gains, heads_map, jnp.asarray(masks))
+
+
+def choose_device(video_tokens, timestep, w_qkv, *rest):
+    videos, fr_dev, _, _ = video_tokens.shape
+    fits = videos == 2 and fr_dev == 8 and w_qkv.shape[1] % (16 * CHUNKS) == 0
+    run = fused_device if fits else per_device
+    return run(video_tokens, timestep, w_qkv, *rest)
+
+
 def solution(mesh):
     placed = (
         P("grp", "frame", "patch", None),
@@ -134,8 +488,9 @@
         P(),
         P(),
     )
+    ring = mesh.shape["patch"] == 8 and mesh.shape["frame"] == 2
     return jax.shard_map(
-        per_device,
+        choose_device if ring else per_device,
         mesh=mesh,
         in_specs=placed,
         out_specs=P("grp", "frame", "patch", None),

time: 269 us -> 111 us (0.41)
  waiting for transfers between devices: 157 us -> 0 us
  Pallas kernels: 0 us -> 101 us
  blocking collectives: 48.4 us -> 0 us
  local copies, waits for them, and re-layouts: 26.3 us -> 5.13 us
  between operations: 14.2 us -> 0.76 us
  matrix products: 13.3 us -> 0 us
  starting transfers between devices: 4 us -> 0 us
    all_gather x4 -> x0, waiting for transfers between devices: 141 us -> none  [the longest x2 125 us: fetch_weights(): lax.all_gather(qkv_rows, 'patch', axis=0, tiled=True)]
    pallas_call x0 -> x1, Pallas kernels: none -> 101 us  [fused_device(): pl.pallas_call(functools.partial(fused_kernel, head_size), out_shape=jax....]
    all_to_all x3 -> x0, blocking collectives: 48.4 us -> none  [the longest x1 40.4 us: spatial(): lax.all_to_all(stacked, 'patch', split_axis=1, concat_axis=3, tiled=True)]
    all_to_all x1 -> x0, waiting for transfers between devices: 15.2 us -> none  [spatial(): lax.all_to_all(attended, 'patch', split_axis=2, concat_axis=0, tiled=True)]
    dot_general x8 -> x0, matrix products: 13.3 us -> none  [the longest x2 7.8 us: per_device(): joint = jnp.dot(mixed, qkv_full, preferred_element_type=jnp.float32)]
    dot_general x1 -> x0, local copies, waits for them, and re-layouts: 6.5 us -> none  [per_device(): joint = jnp.dot(mixed, qkv_full, preferred_element_type=jnp.float32)]
    reshape x11 -> x0, local copies, waits for them, and re-layouts: 5.39 us -> none  [the longest x1 2.19 us: per_device(): joint = joint.reshape(rows, 3, heads, head_size)]
    slice x10 -> x0, local copies, waits for them, and re-layouts: 5.09 us -> none  [the longest x2 3.08 us: per_device(): qkv_full, out_full = fetch_weights(w_qkv[layer], w_out[layer])]
  transfers between devices with their start and end apart: 5 -> 0, of which waited for: 4 -> 0; matrix products, arithmetic and copies ran while one was open for 15% -> 0% of each run, Pallas kernels for 0% -> 0%
where the time goes in v1:
time: 111 us; the launch traced here: 110 us
  Pallas kernels  101 us (91%)
  local copies, waits for them, and re-layouts  5.13 us (5%)
  other arithmetic  3.79 us (3%)
    pallas_call x1, Pallas kernels, fused_device(): pl.pallas_call(functools.partial(fused_kernel, head_size), out_shape=jax....  101 us
    concatenate x1, other arithmetic, fused_device(): joined = jnp.concatenate([w_qkv, w_out.transpose(0, 2, 1)], axis=2)  2.27 us

profile of v1, /device:TPU:0, one launch (start us, length us, event | category | flops | bytes accessed | tf_op | source)
XLA Modules:
  0.0 110.3 jit_solution(519357900136259257)
XLA Ops:
  0.0 0.0 copy-start
  0.8 0.1 pad_maximum_fusion.1
  0.9 0.7 tile.4
  1.6 0.7 tile.10.gain_ref
  2.2 1.4 %copy_add_fusion.par_ref = f32[2,3,1152]{2,1,0:T(4,128)} fusion(f32[2,3,1152]{2,0,1:T(2,128)} %param.14, f32[2,3,1152]{2,0,1:T(2,128)} %param.15, f32[1152]{0:T(1024)S(1)} %pad_maximum_fusion.1), kind=kLoop, calls=%fused_computation.1 | loop fusion | flops 13824 | bytes 87552 | tf_op jit(solution)/shard_map/add | solution.py:424
  3.6 1.9 %copy.12.x_ref = bf16[2,8,10,1152]{3,2,1,0:T(8,128)(2,1)} copy(bf16[2,8,10,1152]{3,1,2,0:T(8,128)(2,1)} %param.9) | data formatting | bytes 737280 | tf_op args[0]
  5.5 0.0 copy-done
  5.5 2.3 %pad_maximum_fusion.w_ref = bf16[2,144,2304]{2,1,0:T(8,128)(2,1)} fusion(bf16[2,144,576]{2,1,0:T(8,128)(2,1)} %bitcast.4, bf16[2,144,1728]{2,1,0:T(8,128)(2,1)S(1)} %copy-done), kind=kLoop, calls=%fused_computation | loop fusion | flops 2654208 | bytes 2654208 | tf_op jit(solution)/shard_map/concatenate | solution.py:426
  7.8 100.6 %blocks.1 = bf16[2,8,10,1152]{3,2,1,0:T(8,128)(2,1)} custom-call(bf16[2,8,10,1152]{3,2,1,0:T(8,128)(2,1)} %copy.12.x_ref, bf16[2,144,2304]{2,1,0:T(8,128)(2,1)} %pad_maximum_fusion.w_ref, f32[2,3,1152]{2,1,0:T(4,128)} %copy_add_fusion.par_ref, f32[2,2,576]{2,1,0:T(2,128)} %tile.10.gain_ref, f32[8,576]{1,0:T(8,128)} %constant.9.clone.heads_ref, ...), custom_call_target="tpu_custom_call" | custom-call | tf_op jit(solution)/shard_map/blocks/pallas_call | solution.py:442
  108.4 1.9 %copy.13 = bf16[2,8,10,1152]{3,1,2,0:T(8,128)(2,1)} copy(bf16[2,8,10,1152]{3,2,1,0:T(8,128)(2,1)} %blocks.1) | data formatting | bytes 737280 | tf_op jit(solution)/shard_map/blocks/pallas_call | solution.py:442
  (1 shorter events, 0.0 us)
Async XLA Ops:
  0.0 5.5 %copy-start = (bf16[2,144,1728]{2,1,0:T(8,128)(2,1)S(1)}, bf16[2,144,1728]{2,1,0:T(8,128)(2,1)}, u32[]{:S(2)}) copy-start(bf16[2,144,1728]{2,1,0:T(8,128)(2,1)} %param.11) | copy-start | bytes 2985988

commit v2 on v1

--- a/solution.py
+++ b/solution.py
@@ -177,7 +177,7 @@
     return (values * wide * gain).astype(jnp.bfloat16)
 
 
-def attend_heads(query, key, value, heads_map, mask, att_ref, head_size):
+def attend_heads(query, key, value, heads_map, mask, att_ref, head_size, between=None):
     feat = query.shape[1]
     att_ref[...] = jnp.zeros_like(att_ref)
     for head in range(feat // head_size):
@@ -189,6 +189,8 @@
         total = jnp.sum(raised, axis=-1, keepdims=True)
         summed = dot_f32(raised.astype(jnp.bfloat16), value[:, low:high] * lanes, (1, 0))
         att_ref[:, low:high] += summed / total
+        if between is not None and head == 3:
+            between()
     return att_ref[...].astype(jnp.bfloat16)
 
 
@@ -196,7 +198,7 @@
     head_size, x_ref, w_ref, par_ref, gain_ref, heads_ref, mask_ref, out_ref,
     wbuf, xin, mid_send, mid_recv, xf, att, res,
     local_sem, in_send, in_recv, ring_send, ring_recv, sib_send, sib_recv,
-    mid_ssem, mid_rsem, fin_send, fin_recv,
+    mid_ssem, mid_rsem, fin_send, fin_recv, twin_send, twin_recv,
 ):
     videos, fr_dev, patch_dev, width = x_ref.shape
     layers, rows, lanes = w_ref.shape
@@ -222,15 +224,18 @@
                     device_id=(grp, lax.rem(me + k, count), lax.rem(core + s, 2)),
                     device_id_type=MESH,
                 )
-    pl.semaphore_wait(barrier, 2 * count - 1)
-
-    def remote(src, dst, send_sem, recv_sem, patch, frame):
+    pl.semaphore_signal(
+        barrier, inc=1, device_id=(1 - grp, me, core), device_id_type=MESH
+    )
+    pl.semaphore_wait(barrier, 2 * count)
+
+    def remote(src, dst, send_sem, recv_sem, patch, frame, to_grp=grp):
         return pltpu.make_async_remote_copy(
             src_ref=src,
             dst_ref=dst,
             send_sem=send_sem,
             recv_sem=recv_sem,
-            device_id=(grp, patch, frame),
+            device_id=(to_grp, patch, frame),
             device_id_type=MESH,
         )
 
@@ -251,67 +256,100 @@
         source = ring_to_patch(lax.rem(pos - direction * step + count, count), count)
         columns = pl.ds(pl.multiple_of(owner_core * half, 128), half)
         if from_input:
-            return w_ref.at[layer, pl.ds(chunk * piece, piece), columns]
+            return w_ref.at[layer, pl.ds(pl.multiple_of(chunk * piece, 16), piece), columns]
         start = pl.multiple_of(source * rows + chunk * piece, 16)
         return wbuf.at[layer, pl.ds(start, piece), columns]
 
-    def ring_copy(layer, step, chunk):
+    def ring_copy(layer, step, slot):
+        chunk = grp if slot == 0 else 2
         return remote(
             block(layer, step, chunk, core, step == 0),
             block(layer, step, chunk, core, False),
-            ring_send.at[layer, step, chunk],
-            ring_recv.at[layer, step, chunk],
+            ring_send.at[layer, step, slot],
+            ring_recv.at[layer, step, slot],
             onward,
             core,
         )
 
-    def arrived(layer, step, chunk):
-        landed = block(layer, step + 1, chunk, core, False)
-        remote(
-            landed,
-            landed,
-            ring_send.at[layer, step, chunk],
-            ring_recv.at[layer, step, chunk],
-            onward,
-            core,
-        ).wait_recv()
-        if step + 1 < count - 1:
-            copy = ring_copy(layer, step + 1, chunk)
+    def ring_start(layer):
+        for slot in range(2):
+            copy = ring_copy(layer, 0, slot)
             copy.start()
             sent.append(copy)
+
+    def to_sibling(layer, step, slot, landed):
         copy = remote(
             landed,
             landed,
-            sib_send.at[layer, step, chunk],
-            sib_recv.at[layer, step, chunk],
+            sib_send.at[layer, step, slot],
+            sib_recv.at[layer, step, slot],
             me,
             sib,
         )
         copy.start()
         sent.append(copy)
 
+    def twin_step(layer, step):
+        landed = block(layer, step + 1, 1 - grp, core, False)
+        remote(
+            landed,
+            landed,
+            twin_send.at[layer, step],
+            twin_recv.at[layer, step],
+            me,
+            core,
+            1 - grp,
+        ).wait_recv()
+        to_sibling(layer, step, 2, landed)
+
     def ring_step(layer, step):
-        for chunk in range(CHUNKS):
-            arrived(layer, step, chunk)
+        for slot in range(2):
+            landed = block(layer, step + 1, grp if slot == 0 else 2, core, False)
+            remote(
+                landed,
+                landed,
+                ring_send.at[layer, step, slot],
+                ring_recv.at[layer, step, slot],
+                onward,
+                core,
+            ).wait_recv()
+            if step + 1 < count - 1:
+                copy = ring_copy(layer, step + 1, slot)
+                copy.start()
+                sent.append(copy)
+            if slot == 0:
+                copy = remote(
+                    landed,
+                    landed,
+                    twin_send.at[layer, step],
+                    twin_recv.at[layer, step],
+                    me,
+                    core,
+                    1 - grp,
+                )
+                copy.start()
+                sent.append(copy)
+            to_sibling(layer, step, slot, landed)
+        if step > 0:
+            twin_step(layer, step - 1)
+        if step == count - 2:
+            twin_step(layer, step)
 
     def sibling_done(layer):
         for step in range(count - 1):
-            for chunk in range(CHUNKS):
+            for slot in range(CHUNKS):
+                chunk = (grp, 2, 1 - grp)[slot]
                 landed = block(layer, step + 1, chunk, sib, False)
                 remote(
                     landed,
                     landed,
-                    sib_send.at[layer, step, chunk],
-                    sib_recv.at[layer, step, chunk],
+                    sib_send.at[layer, step, slot],
+                    sib_recv.at[layer, step, slot],
                     me,
                     sib,
                 ).wait_recv()
 
-    for layer in range(layers):
-        for chunk in range(CHUNKS):
-            copy = ring_copy(layer, 0, chunk)
-            copy.start()
-            sent.append(copy)
+    ring_start(0)
     own_w.start()
 
     heads_map = heads_ref[...]
@@ -339,12 +377,16 @@
     mixed = norm_tokens(xf[...], par_ref[0])
     for step in range(count - 1):
         ring_step(0, step)
+        if step == count - 3:
+            ring_start(1)
     own_w.wait()
     sibling_done(0)
     query, key, value = project(0, mixed)
     ring_step(1, 0)
-    attended = attend_heads(query, key, value, heads_map, mask_ref[0], att, head_size)
-    ring_step(1, 1)
+    attended = attend_heads(
+        query, key, value, heads_map, mask_ref[0], att, head_size, lambda: ring_step(1, 1)
+    )
+    ring_step(1, 2)
     xf[...] = update(0, xf[...], attended)
 
     frame = core * count + me
@@ -368,7 +410,7 @@
                 )
                 copy.start()
                 sent.append(copy)
-    for step in range(2, count - 1):
+    for step in range(3, count - 1):
         ring_step(1, step)
     own_mid.wait()
     for s in range(2):
@@ -442,7 +484,7 @@
     return pl.pallas_call(
         functools.partial(fused_kernel, head_size),
         out_shape=jax.ShapeDtypeStruct(video_tokens.shape, bf16),
-        in_specs=[vmem] * 6,
+        in_specs=[pl.BlockSpec(memory_space=pl.ANY)] + [vmem] * 5,
         out_specs=vmem,
         scratch_shapes=[
             pltpu.VMEM((layers, count * rows, lanes), bf16),
@@ -455,14 +497,16 @@
             dma((4,)),
             dma((count,)),
             dma((count,)),
-            dma(ring),
-            dma(ring),
+            dma(ring[:2] + (2,)),
+            dma(ring[:2] + (2,)),
             dma(ring),
             dma(ring),
             dma((2 * count,)),
             dma((2 * count,)),
             dma,
             dma,
+            dma((layers, count - 1)),
+            dma((layers, count - 1)),
         ],
         compiler_params=pltpu.CompilerParams(
             collective_id=0, has_side_effects=True, vmem_limit_bytes=56 * 1024 * 1024
@@ -488,7 +532,7 @@
         P(),
         P(),
     )
-    ring = mesh.shape["patch"] == 8 and mesh.shape["frame"] == 2
+    ring = (mesh.shape["grp"], mesh.shape["patch"], mesh.shape["frame"]) == (2, 8, 2)
     return jax.shard_map(
         choose_device if ring else per_device,
         mesh=mesh,

time: 111 us -> 107 us (0.964)
  Pallas kernels: 101 us -> 97.3 us
    pallas_call x1, Pallas kernels: 101 us -> 97.3 us  [fused_device(): pl.pallas_call(functools.partial(fused_kernel, head_size), out_shape=jax....]
where the time goes in v2:
time: 107 us
  Pallas kernels  97.3 us (91%)
  local copies, waits for them, and re-layouts  5.13 us (5%)
  other arithmetic  3.79 us (4%)
    pallas_call x1, Pallas kernels, fused_device(): pl.pallas_call(functools.partial(fused_kernel, head_size), out_shape=jax....  97.3 us
    concatenate x1, other arithmetic, fused_device(): joined = jnp.concatenate([w_qkv, w_out.transpose(0, 2, 1)], axis=2)  2.27 us

profile of v2, /device:TPU:0, one launch (start us, length us, event | category | flops | bytes accessed | tf_op | source)
XLA Modules:
  0.0 107.0 jit_solution(17410780903504995499)
XLA Ops:
  0.0 0.0 copy-start
  0.8 0.1 pad_maximum_fusion.1
  0.9 0.7 tile.4
  1.6 0.7 tile.10.gain_ref
  2.2 1.4 %copy_add_fusion.par_ref = f32[2,3,1152]{2,1,0:T(4,128)} fusion(f32[2,3,1152]{2,0,1:T(2,128)} %param.14, f32[2,3,1152]{2,0,1:T(2,128)} %param.15, f32[1152]{0:T(1024)S(1)} %pad_maximum_fusion.1), kind=kLoop, calls=%fused_computation.1 | loop fusion | flops 13824 | bytes 87552 | tf_op jit(solution)/shard_map/add | solution.py:466
  3.6 1.9 %copy.12.x_ref = bf16[2,8,10,1152]{3,2,1,0:T(8,128)(2,1)} copy(bf16[2,8,10,1152]{3,1,2,0:T(8,128)(2,1)} %param.9) | data formatting | bytes 737280 | tf_op args[0]
  5.5 0.0 copy-done
  5.5 2.3 %pad_maximum_fusion.w_ref = bf16[2,144,2304]{2,1,0:T(8,128)(2,1)} fusion(bf16[2,144,576]{2,1,0:T(8,128)(2,1)} %bitcast.4, bf16[2,144,1728]{2,1,0:T(8,128)(2,1)S(1)} %copy-done), kind=kLoop, calls=%fused_computation | loop fusion | flops 2654208 | bytes 2654208 | tf_op jit(solution)/shard_map/concatenate | solution.py:468
  7.8 97.3 %blocks.1 = bf16[2,8,10,1152]{3,2,1,0:T(8,128)(2,1)} custom-call(bf16[2,8,10,1152]{3,2,1,0:T(8,128)(2,1)} %copy.12.x_ref, bf16[2,144,2304]{2,1,0:T(8,128)(2,1)} %pad_maximum_fusion.w_ref, f32[2,3,1152]{2,1,0:T(4,128)} %copy_add_fusion.par_ref, f32[2,2,576]{2,1,0:T(2,128)} %tile.10.gain_ref, f32[8,576]{1,0:T(8,128)} %constant.9.clone.heads_ref, ...), custom_call_target="tpu_custom_call" | custom-call | tf_op jit(solution)/shard_map/blocks/pallas_call | solution.py:484
  105.2 1.9 %copy.13 = bf16[2,8,10,1152]{3,1,2,0:T(8,128)(2,1)} copy(bf16[2,8,10,1152]{3,2,1,0:T(8,128)(2,1)} %blocks.1) | data formatting | bytes 737280 | tf_op jit(solution)/shard_map/blocks/pallas_call | solution.py:484
  (1 shorter events, 0.0 us)
Async XLA Ops:
  0.0 5.5 %copy-start = (bf16[2,144,1728]{2,1,0:T(8,128)(2,1)S(1)}, bf16[2,144,1728]{2,1,0:T(8,128)(2,1)}, u32[]{:S(2)}) copy-start(bf16[2,144,1728]{2,1,0:T(8,128)(2,1)} %param.11) | copy-start | bytes 2985988
